TPU v7x, 32 devices: a whole 2x2x4 slice. The times are simulated.
32 devices in a mesh: dp: 8 (over y, x, core), seq: 4 (over z).
Axes of the slice: x: 2, y: 2, z: 4, core: 2. Of those that a mesh axis runs over, the one named last changes fastest.
Arguments:
- inputs: bfloat16 [16, 576, 1152], P('dp', 'seq'), may hold values from -90 to 90
- cotangent: bfloat16 [16, 576, 1152], P('dp', 'seq'), may hold values from -6 to 6
- ln1_gain: bfloat16 [1152], P(('dp', 'seq')), may hold values from 0.099609375 to 1.8984375
- ln1_bias: bfloat16 [1152], P(('dp', 'seq')), may hold values from -3 to 3
- qkv_weight: bfloat16 [1152, 3456], P(('dp', 'seq')), may hold values from -0.1875 to 0.1875
- qv_bias: bfloat16 [2, 1152], P(None, ('dp', 'seq')), may hold values from -3 to 3
- out_weight: bfloat16 [1152, 1152], P(('dp', 'seq')), may hold values from -2.5 to 2.5
- out_bias: bfloat16 [1152], P(('dp', 'seq')), may hold values from -3 to 3
- ln2_gain: bfloat16 [1152], P(('dp', 'seq')), may hold values from 0.099609375 to 1.8984375
- ln2_bias: bfloat16 [1152], P(('dp', 'seq')), may hold values from -3 to 3
- up_weight: bfloat16 [1152, 4304], P(('dp', 'seq')), may hold values from -0.1875 to 0.1875
- up_bias: bfloat16 [4304], replicated, may hold values from -3 to 3
- down_weight: bfloat16 [4304, 1152], P(None, ('dp', 'seq')), may hold values from -0.09375 to 0.09375
- down_bias: bfloat16 [1152], P(('dp', 'seq')), may hold values from -3 to 3
Outputs:
- output: bfloat16 [16, 576, 1152], P('dp', 'seq')
- input_grad: bfloat16 [16, 576, 1152], P('dp', 'seq')
- ln1_gain_grad: float32 [1152], P(('dp', 'seq'))
- ln1_bias_grad: float32 [1152], P(('dp', 'seq'))
- qkv_weight_grad: float32 [1152, 3456], P(('dp', 'seq'))
- qv_bias_grad: float32 [2, 1152], P(None, ('dp', 'seq'))
- out_weight_grad: float32 [1152, 1152], P(('dp', 'seq'))
- out_bias_grad: float32 [1152], P(('dp', 'seq'))
- ln2_gain_grad: float32 [1152], P(('dp', 'seq'))
- ln2_bias_grad: float32 [1152], P(('dp', 'seq'))
- up_weight_grad: float32 [1152, 4304], P(('dp', 'seq'))
- up_bias_grad: float32 [4304], replicated
- down_weight_grad: float32 [4304, 1152], P(None, ('dp', 'seq'))
- down_bias_grad: float32 [1152], P(('dp', 'seq'))
All inputs are finite; a program needn't handle non-finite values.
Results may differ from a plain program's by a relative error of at most 0.012.
The roundings to bfloat16 on the way count: a program that leaves them out, or rounds other values in their place, can miss the bound.
Values may be sent and summed in bfloat16 or wider, within the bound.
No kernel may reach another device: no remote copies, remote signals or barrier semaphores. Data moves between devices by JAX's collectives and lax.ppermute only.
A program may use at most 320 MiB of HBM per device.

v0:
```python
import jax
import jax.numpy as jnp
from jax import lax
from jax.sharding import PartitionSpec as P

HEADS = 16
HEAD = 72
EPS = 1e-06
GELU_C = 0.7978845608028654
GELU_A = 0.044715


def layer_norm(values, gain_row, offset):
    average = jnp.mean(values, axis=-1, keepdims=True)
    centred = values - average
    variance = jnp.mean(centred * centred, axis=-1, keepdims=True)
    inverse = lax.rsqrt(variance + EPS)
    normed = centred * inverse
    return (normed, inverse, normed * gain_row + offset)


def norm_back(grad_normed, normed, inverse):
    mean_grad = jnp.mean(grad_normed, axis=-1, keepdims=True)
    mean_mixed = jnp.mean(grad_normed * normed, axis=-1, keepdims=True)
    return inverse * (grad_normed - mean_grad - normed * mean_mixed)


def gelu_parts(pre_act):
    inner_arg = GELU_C * (pre_act + GELU_A * pre_act * pre_act * pre_act)
    tangent = jnp.tanh(inner_arg)
    gelu_value = 0.5 * pre_act * (1.0 + tangent)
    slopes = 0.5 * (1.0 + tangent) + 0.5 * pre_act * (1.0 - tangent * tangent) * GELU_C * (
        1.0 + 3.0 * GELU_A * pre_act * pre_act
    )
    return (gelu_value, slopes)


def contract_rows(left, right):
    return lax.dot_general(
        left, right, (((0,), (0,)), ((), ())), preferred_element_type=jnp.float32
    )


def contract_cols(left, right):
    return lax.dot_general(
        left, right, (((1,), (1,)), ((), ())), preferred_element_type=jnp.float32
    )


def attend_block(queries, key_rows, value_rows, scaling, block_rows):
    length, head_count, head_width = queries.shape

    def one_block(block_index):
        query_block = lax.dynamic_slice_in_dim(queries, block_index * block_rows, block_rows, 0)
        scores = (
            jnp.einsum("qhd,khd->hqk", query_block, key_rows, preferred_element_type=jnp.float32)
            * scaling
        )
        row_top = jnp.max(scores, axis=-1, keepdims=True)
        log_total = row_top + jnp.log(jnp.sum(jnp.exp(scores - row_top), axis=-1, keepdims=True))
        weights_b = jnp.exp(scores - log_total).astype(jnp.bfloat16)
        attended = jnp.einsum(
            "hqk,khd->qhd", weights_b, value_rows, preferred_element_type=jnp.float32
        ).astype(jnp.bfloat16)
        return (attended, log_total[:, :, 0])

    attended, log_total = lax.map(one_block, jnp.arange(length // block_rows, dtype=jnp.int32))
    return (
        attended.reshape(length, head_count, head_width),
        jnp.moveaxis(log_total, 0, 1).reshape(head_count, length),
    )


def attend_back(
    queries, key_rows, value_rows, attended, log_total, grad_attended, scaling, block_rows
):
    length, head_count, head_width = queries.shape
    row_delta = jnp.sum(grad_attended.astype(jnp.float32) * attended.astype(jnp.float32), axis=-1)

    def one_block(running, block_index):
        key_grad, value_grad = running
        row_start = block_index * block_rows
        query_block = lax.dynamic_slice_in_dim(queries, row_start, block_rows, 0)
        grad_block = lax.dynamic_slice_in_dim(grad_attended, row_start, block_rows, 0)
        log_block = lax.dynamic_slice_in_dim(log_total, row_start, block_rows, 1)
        delta_block = lax.dynamic_slice_in_dim(row_delta, row_start, block_rows, 0)
        scores = (
            jnp.einsum("qhd,khd->hqk", query_block, key_rows, preferred_element_type=jnp.float32)
            * scaling
        )
        probabilities = jnp.exp(scores - log_block[:, :, None])
        value_grad = value_grad + jnp.einsum(
            "hqk,qhd->khd",
            probabilities.astype(jnp.bfloat16),
            grad_block,
            preferred_element_type=jnp.float32,
        )
        prob_grad = jnp.einsum(
            "qhd,khd->hqk", grad_block, value_rows, preferred_element_type=jnp.float32
        )
        score_grad = (
            probabilities * (prob_grad - jnp.transpose(delta_block)[:, :, None]) * scaling
        ).astype(jnp.bfloat16)
        query_grad = jnp.einsum(
            "hqk,khd->qhd", score_grad, key_rows, preferred_element_type=jnp.float32
        )
        key_grad = key_grad + jnp.einsum(
            "hqk,qhd->khd", score_grad, query_block, preferred_element_type=jnp.float32
        )
        return ((key_grad, value_grad), query_grad)

    zero_grad = jnp.zeros((length, head_count, head_width), jnp.float32)
    (key_grad, value_grad), query_grad = lax.scan(
        one_block, (zero_grad, zero_grad), jnp.arange(length // block_rows, dtype=jnp.int32)
    )
    return (query_grad.reshape(length, head_count, head_width), key_grad, value_grad)


def local(
    inputs,
    cotangent,
    ln1_gain,
    ln1_bias,
    qkv_weight,
    qv_bias,
    out_weight,
    out_bias,
    ln2_gain,
    ln2_bias,
    up_weight,
    up_bias,
    down_weight,
    down_bias,
):
    images, tok_rows, model_width = inputs.shape
    groups = lax.axis_size("seq")
    head_share = HEADS // groups
    length = tok_rows * groups
    row_count = images * tok_rows
    scaling = HEAD ** (-0.5)
    block_rows = min(576, length)
    attn_set = (
        lax.all_gather(ln1_gain, ("dp", "seq"), axis=0, tiled=True),
        lax.all_gather(ln1_bias, ("dp", "seq"), axis=0, tiled=True),
        lax.all_gather(qkv_weight, ("dp", "seq"), axis=0, tiled=True),
        lax.all_gather(qv_bias, ("dp", "seq"), axis=1, tiled=True),
        lax.all_gather(out_weight, ("dp", "seq"), axis=0, tiled=True),
        lax.all_gather(out_bias, ("dp", "seq"), axis=0, tiled=True),
    )
    gain_one, shift_one, qkv_full, qv_full, out_full, out_bias_full = attn_set
    gain_one_f = gain_one.astype(jnp.float32)
    input_f = inputs.reshape(row_count, model_width).astype(jnp.float32)
    normed1, inverse1, shifted1 = layer_norm(input_f, gain_one_f, shift_one.astype(jnp.float32))
    attn_input = shifted1.astype(jnp.bfloat16)
    bias_full = jnp.concatenate(
        [
            qv_full[0].astype(jnp.float32),
            jnp.zeros((model_width,), jnp.float32),
            qv_full[1].astype(jnp.float32),
        ]
    )
    projected = (
        jnp.dot(attn_input, qkv_full, preferred_element_type=jnp.float32) + bias_full
    ).astype(jnp.bfloat16)
    projected = projected.reshape(images, tok_rows, 3, model_width)
    by_heads = lax.all_to_all(projected, "seq", split_axis=3, concat_axis=1, tiled=True)

    def attend_one(one_image):
        queries = one_image[:, 0].reshape(length, head_share, HEAD)
        key_rows = one_image[:, 1].reshape(length, head_share, HEAD)
        value_rows = one_image[:, 2].reshape(length, head_share, HEAD)
        return attend_block(queries, key_rows, value_rows, scaling, block_rows)

    attended_heads, log_totals = lax.map(attend_one, by_heads)
    attended_tok = lax.all_to_all(
        attended_heads.reshape(images, length, head_share * HEAD),
        "seq",
        split_axis=1,
        concat_axis=2,
        tiled=True,
    )
    attended_flat = attended_tok.reshape(row_count, model_width)
    hidden = (
        input_f
        + jnp.dot(attended_flat, out_full, preferred_element_type=jnp.float32)
        + out_bias_full.astype(jnp.float32)
    )
    mlp_set = (
        lax.all_gather(ln2_gain, ("dp", "seq"), axis=0, tiled=True),
        lax.all_gather(ln2_bias, ("dp", "seq"), axis=0, tiled=True),
        lax.all_gather(up_weight, ("dp", "seq"), axis=0, tiled=True),
        lax.all_gather(down_weight, ("dp", "seq"), axis=1, tiled=True),
        lax.all_gather(down_bias, ("dp", "seq"), axis=0, tiled=True),
    )
    gain_two, shift_two, up_full, down_full, down_bias_full = mlp_set
    normed2, inverse2, shifted2 = layer_norm(
        hidden, gain_two.astype(jnp.float32), shift_two.astype(jnp.float32)
    )
    mlp_input = shifted2.astype(jnp.bfloat16)
    pre_act = jnp.dot(mlp_input, up_full, preferred_element_type=jnp.float32) + up_bias.astype(
        jnp.float32
    )
    gelu_value, slopes = gelu_parts(pre_act)
    gelu_out = gelu_value.astype(jnp.bfloat16)
    result = (
        hidden
        + jnp.dot(gelu_out, down_full, preferred_element_type=jnp.float32)
        + down_bias_full.astype(jnp.float32)
    ).astype(jnp.bfloat16)
    gain_two_back, up_back, down_back = (
        lax.all_gather(ln2_gain, ("dp", "seq"), axis=0, tiled=True),
        lax.all_gather(up_weight, ("dp", "seq"), axis=0, tiled=True),
        lax.all_gather(down_weight, ("dp", "seq"), axis=1, tiled=True),
    )
    grad_rows = cotangent.reshape(row_count, model_width)
    grad_f = grad_rows.astype(jnp.float32)
    down_bias_grad = jnp.sum(grad_f, axis=0)
    down_weight_grad = contract_rows(gelu_out, grad_rows)
    gelu_grad = contract_cols(grad_rows, down_back)
    pre_grad = (gelu_grad * slopes).astype(jnp.bfloat16)
    up_weight_grad = contract_rows(mlp_input, pre_grad)
    up_bias_part = jnp.sum(pre_grad.astype(jnp.float32), axis=0)
    mlp_in_grad = contract_cols(pre_grad, up_back)
    ln2_gain_grad = jnp.sum(mlp_in_grad * normed2, axis=0)
    ln2_bias_grad = jnp.sum(mlp_in_grad, axis=0)
    hidden_grad = grad_f + norm_back(
        mlp_in_grad * gain_two_back.astype(jnp.float32), normed2, inverse2
    )
    mlp_owned = (
        lax.psum_scatter(ln2_gain_grad, ("dp", "seq"), scatter_dimension=0, tiled=True),
        lax.psum_scatter(ln2_bias_grad, ("dp", "seq"), scatter_dimension=0, tiled=True),
        lax.psum_scatter(up_weight_grad, ("dp", "seq"), scatter_dimension=0, tiled=True),
        lax.psum_scatter(down_weight_grad, ("dp", "seq"), scatter_dimension=1, tiled=True),
        lax.psum_scatter(down_bias_grad, ("dp", "seq"), scatter_dimension=0, tiled=True),
    )
    up_bias_total = lax.psum(up_bias_part, ("dp", "seq"))
    gain_one_back, qkv_back, out_back = (
        lax.all_gather(ln1_gain, ("dp", "seq"), axis=0, tiled=True),
        lax.all_gather(qkv_weight, ("dp", "seq"), axis=0, tiled=True),
        lax.all_gather(out_weight, ("dp", "seq"), axis=0, tiled=True),
    )
    out_bias_grad = jnp.sum(hidden_grad, axis=0)
    hidden_grad_b = hidden_grad.astype(jnp.bfloat16)
    out_weight_grad = contract_rows(attended_flat, hidden_grad_b)
    attended_grad = (
        contract_cols(hidden_grad_b, out_back)
        .astype(jnp.bfloat16)
        .reshape(images, tok_rows, model_width)
    )
    grad_heads = lax.all_to_all(attended_grad, "seq", split_axis=2, concat_axis=1, tiled=True)

    def attend_back_one(pieces):
        heads_in, attended_in, logs_in, grads_in = pieces
        queries = heads_in[:, 0].reshape(length, head_share, HEAD)
        key_rows = heads_in[:, 1].reshape(length, head_share, HEAD)
        value_rows = heads_in[:, 2].reshape(length, head_share, HEAD)
        grads_split = grads_in.reshape(length, head_share, HEAD)
        query_grad, key_grad, value_grad = attend_back(
            queries, key_rows, value_rows, attended_in, logs_in, grads_split, scaling, block_rows
        )
        flat_width = head_share * HEAD
        return jnp.stack(
            [
                query_grad.reshape(length, flat_width),
                key_grad.reshape(length, flat_width),
                value_grad.reshape(length, flat_width),
            ],
            axis=1,
        ).astype(jnp.bfloat16)

    stacked_grads = lax.map(attend_back_one, (by_heads, attended_heads, log_totals, grad_heads))
    projected_grad = lax.all_to_all(
        stacked_grads, "seq", split_axis=1, concat_axis=3, tiled=True
    ).reshape(row_count, 3 * model_width)
    qkv_weight_grad = contract_rows(attn_input, projected_grad)
    projected_f = projected_grad.astype(jnp.float32)
    qv_bias_grad = jnp.stack(
        [
            jnp.sum(projected_f[:, :model_width], axis=0),
            jnp.sum(projected_f[:, 2 * model_width :], axis=0),
        ]
    )
    attn_in_grad = contract_cols(projected_grad, qkv_back)
    ln1_gain_grad = jnp.sum(attn_in_grad * normed1, axis=0)
    ln1_bias_grad = jnp.sum(attn_in_grad, axis=0)
    input_grad = (
        hidden_grad + norm_back(attn_in_grad * gain_one_back.astype(jnp.float32), normed1, inverse1)
    ).astype(jnp.bfloat16)
    attn_owned = (
        lax.psum_scatter(ln1_gain_grad, ("dp", "seq"), scatter_dimension=0, tiled=True),
        lax.psum_scatter(ln1_bias_grad, ("dp", "seq"), scatter_dimension=0, tiled=True),
        lax.psum_scatter(qkv_weight_grad, ("dp", "seq"), scatter_dimension=0, tiled=True),
        lax.psum_scatter(qv_bias_grad, ("dp", "seq"), scatter_dimension=1, tiled=True),
        lax.psum_scatter(out_weight_grad, ("dp", "seq"), scatter_dimension=0, tiled=True),
        lax.psum_scatter(out_bias_grad, ("dp", "seq"), scatter_dimension=0, tiled=True),
    )
    owned_all = attn_owned + mlp_owned
    return (
        result.reshape(images, tok_rows, model_width),
        input_grad.reshape(images, tok_rows, model_width),
        owned_all[0],
        owned_all[1],
        owned_all[2],
        owned_all[3],
        owned_all[4],
        owned_all[5],
        owned_all[6],
        owned_all[7],
        owned_all[8],
        up_bias_total,
        owned_all[9],
        owned_all[10],
    )


def solution(mesh):
    in_specs = (
        P("dp", "seq", None),
        P("dp", "seq", None),
        P(("dp", "seq")),
        P(("dp", "seq")),
        P(("dp", "seq"), None),
        P(None, ("dp", "seq")),
        P(("dp", "seq"), None),
        P(("dp", "seq")),
        P(("dp", "seq")),
        P(("dp", "seq")),
        P(("dp", "seq"), None),
        P(),
        P(None, ("dp", "seq")),
        P(("dp", "seq")),
    )
    out_specs = (
        P("dp", "seq", None),
        P("dp", "seq", None),
        P(("dp", "seq")),
        P(("dp", "seq")),
        P(("dp", "seq"), None),
        P(None, ("dp", "seq")),
        P(("dp", "seq"), None),
        P(("dp", "seq")),
        P(("dp", "seq")),
        P(("dp", "seq")),
        P(("dp", "seq"), None),
        P(),
        P(None, ("dp", "seq")),
        P(("dp", "seq")),
    )
    return jax.shard_map(local, mesh=mesh, in_specs=in_specs, out_specs=out_specs, check_vma=False)
```

profile of v0, /device:TPU:19, one launch (start us, length us, event | category | flops | bytes accessed | tf_op | source)
XLA Modules:
  0.0 2467.8 jit_solution(2320902800671834990)
XLA Ops:
  17.9 41.7 %all-reduce.22 = (bf16[1152]{0:T(1024)(128)(2,1)S(1)}, bf16[1152]{0:T(1024)(128)(2,1)S(1)}, bf16[1152]{0:T(1024)(128)(2,1)}, bf16[1152]{0:T(1024)(128)(2,1)}, bf...) all-reduce(bf16[1152]{0:T(1024)(128)(2,1)S(1)} %dynamic-update-slic, ...), channel_id=1, replica_groups=mesh['dp'=8,'seq'=4] {'dp','seq'}, use_global_device_ids=true, to_apply=%add.1 | all-reduce | flops 6912 | bytes 27648
  59.7 62.3 %all-gather.1 = bf16[32,36,2]{1,2,0:T(2,128)(2,1)S(1)} all-gather(bf16[1,36,2]{1,2,0:T(2,128)(2,1)} %bitcast.199), channel_id=1, replica_groups=mesh['dp'=8,'seq'=4] {'dp','seq'}, dimensions={0}, use_global_device_ids=true | all-gather | bytes 4752 | tf_op jit(solution)/shard_map/all_gather | solution.py:146
  123.6 12.4 reshape.265
  145.4 12.5 copy.73
  163.6 110.8 %all-to-all-done = bf16[2,144,3,1152]{1,0,2,3:T(2,128)(2,1)} async-done(((bf16[2,144,3,1152]{1,0,2,3:T(2,128)(2,1)}), bf16[2,144,3,1152]{1,0,2,3:T(2,128)(2,1)}, u32[]{:S(2)}, u32[]{:S(2)}) %all-to-all-start) | async-done | bytes 1990688 | tf_op jit(solution)/shard_map/all_to_all | solution.py:166
  274.4 12.5 copy.89
  294.1 9.9 while.18
  327.2 14.6 reshape.271
  341.8 51.9 %all-gather.16.cloned.1.call-done = bf16[32,36,4304]{2,1,0:T(8,128)(2,1)} async-done(((bf16[1,36,4304]{2,1,0:T(8,128)(2,1)}), bf16[32,36,4304]{2,1,0:T(8,128)(2,1)}) %all-gather.16.cloned.1.call-update) | async-done | bytes 9916432 | tf_op jit(solution)/shard_map/all_gather | solution.py:192
  393.7 14.6 reshape.273
  423.7 9.9 fusion.40
  462.1 494.5 %fusion.3 = f32[4304,40]{0,1:T(8,128)} fusion(f32[4304,1152]{0,1:T(8,128)} %fusion.40), kind=kCustom, calls=%all-reduce-scatter.3 | all-reduce-scatter fusion | flops 5509121 | bytes 20521472
  976.6 23.9 while.19
  1014.9 11.3 fusion.39
  1026.2 9.9 fusion.30
  1043.6 15.5 concatenate.15
  1060.0 18.3 all-to-all-done.3
  1094.7 1056.8 %fusion.42 = (f32[48,3456]{1,0:T(8,128)S(1)}, f32[48,1152]{1,0:T(8,128)S(1)}, f32[40,4304]{1,0:T(8,128)}) fusion(f32[1152,3456]{1,0:T(8,128)} %fusion.48, f32[1152,1152]{1,0:T(8,128)} %fusion.34, f32[1152,4304]{1,0:T(8,128)} %fusion.39), kind=kCustom, calls=%all-reduce-scatter.4 | all-reduce-scatter fusion | flops 12587010 | bytes 42639872
  2175.5 27.1 %collective-permute-done.15 = f32[36,1152]{1,0:T(8,128)S(1)} collective-permute-done((f32[36,1152]{1,0:T(8,128)S(1)}, f32[36,1152]{1,0:T(8,128)S(1)}, u32[]{:S(2)}, u32[]{:S(2)}) %collective-permute-start.15) | collective-permute-done | bytes 165920
  2209.4 61.9 %all-reduce.21 = (f32[1152]{0:T(1024)}, f32[1152]{0:T(1024)}, f32[2,1152]{1,0:T(2,128)}, f32[1152]{0:T(1024)}, f32[1152]{0:T(1024)}, /*index=5*/f32[1152]{0:T(1024)}, f32[4304]{0:T(1024)}, f32[1152]{0:T(1024)}) all-reduce(f32[1152]{0:T(1024)} %get-tuple-element.169, ...), channel_id=2, replica_groups=mesh['dp'=8,'seq'=4] {'dp','seq'}, use_global_device_ids=true, to_apply=%region_16.17.clone | all-reduce | flops 13520 | bytes 108160
  2347.2 31.3 %collective-permute-done.1 = f32[48,3456]{1,0:T(8,128)} collective-permute-done((f32[48,3456]{1,0:T(8,128)S(1)}, f32[48,3456]{1,0:T(8,128)}, u32[]{:S(2)}, u32[]{:S(2)}) %collective-permute-start.1) | collective-permute-done | bytes 663584
  2380.7 26.2 %collective-permute-done = f32[48,3456]{1,0:T(8,128)} collective-permute-done((f32[48,3456]{1,0:T(8,128)S(1)}, f32[48,3456]{1,0:T(8,128)}, u32[]{:S(2)}, u32[]{:S(2)}) %collective-permute-start) | collective-permute-done | bytes 663584
  2406.9 36.8 %concatenate.12 = f32[420,3456]{1,0:T(8,128)} concatenate(f32[36,3456]{1,0:T(8,128)} %collective-permute-done.7, f32[48,3456]{1,0:T(8,128)} %copy-done.17, f32[48,3456]{1,0:T(8,128)} %collective-permute-done.5, f32[48,3456]{1,0:T(8,128)} %collective-permute-done.4, f32[48,3456]{1,0:T(8,128)} %collective-permute-done.3, f32[48,3456]{1,0:T(8,128)} %collective-permute-done.2, ...), dimensions={0} | concatenate | bytes 11612160
  2445.6 14.5 concatenate.14
  (283 shorter events, 305.3 us)
Async XLA Ops:
  7.2 116.4 %all-gather.10.cloned.1.call-start = ((), (), s32[]{:S(2)}) async-start(), calls=%async_computation.4 | async-start | bytes 9123840 | tf_op jit(solution)/shard_map/all_gather | solution.py:145
  7.9 314.2 %all-gather.12.cloned.1.call-start = ((), (), s32[]{:S(2)}) async-start(), calls=%async_computation.5 | async-start | bytes 3041280 | tf_op jit(solution)/shard_map/all_gather | solution.py:147
  8.7 318.6 %all-gather.14.cloned.1.call-start = ((), (), s32[]{:S(2)}) async-start(), calls=%async_computation.6 | async-start | bytes 11489280 | tf_op jit(solution)/shard_map/all_gather | solution.py:191
  9.4 384.3 %all-gather.16.cloned.1.call-start = ((), (), s32[]{:S(2)}) async-start(), calls=%async_computation.7 | async-start | bytes 11489280 | tf_op jit(solution)/shard_map/all_gather | solution.py:192
  157.9 116.5 %all-to-all-start = ((bf16[2,144,3,1152]{1,0,2,3:T(2,128)(2,1)}), bf16[2,144,3,1152]{1,0,2,3:T(2,128)(2,1)}, u32[]{:S(2)}, u32[]{:S(2)}) async-start(bf16[2,144,3,1152]{1,0,2,3:T(2,128)(2,1)} %copy.73), calls=%async_computation | async-start | bytes 7077888 | tf_op jit(solution)/shard_map/all_to_all | solution.py:166
  307.2 101.1 %all-to-all-start.1 = ((bf16[2,576,288]{2,0,1:T(2,128)(2,1)}), bf16[2,576,288]{2,0,1:T(2,128)(2,1)}, u32[]{:S(2)}, u32[]{:S(2)}) async-start(bf16[2,576,288]{2,0,1:T(2,128)(2,1)} %copy.77), calls=%async_computation.1 | async-start | bytes 1769472 | tf_op jit(solution)/shard_map/all_to_all | solution.py:175
  457.1 510.2 %all-to-all-start.2 = ((bf16[2,144,1152]{1,0,2:T(2,128)(2,1)}), bf16[2,144,1152]{1,0,2:T(2,128)(2,1)}, u32[]{:S(2)}, u32[]{:S(2)}) async-start(bf16[2,144,1152]{1,0,2:T(2,128)(2,1)} %copy.80), calls=%async_computation.2 | async-start | bytes 2359296 | tf_op jit(solution)/shard_map/all_to_all | solution.py:250
  956.6 86.3 %collective-permute-start.22 = (f32[4304,40]{0,1:T(8,128)}, f32[4304,40]{0,1:T(8,128)}, u32[]{:S(2)}, u32[]{:S(2)}) collective-permute-start(f32[4304,40]{0,1:T(8,128)} %fusion.3), channel_id=1, source_target_pairs={{0,3},{1,4},{2,5},{3,6},{4,7},{5,8},{6,9},{7,10},{8,11},{9,12},{10... | collective-permute-start | bytes 2065928
  961.0 81.9 %collective-permute-start.21 = (f32[4304,40]{0,1:T(8,128)}, f32[4304,40]{0,1:T(8,128)}, u32[]{:S(2)}, u32[]{:S(2)}) collective-permute-start(f32[4304,40]{0,1:T(8,128)} %fusion.3), channel_id=1, source_target_pairs={{0,2},{1,3},{2,4},{3,5},{4,6},{5,7},{6,8},{7,9},{8,10},{9,11},{10,... | collective-permute-start | bytes 2065928
  965.3 78.3 %collective-permute-start.20 = (f32[4304,40]{0,1:T(8,128)}, f32[4304,40]{0,1:T(8,128)}, u32[]{:S(2)}, u32[]{:S(2)}) collective-permute-start(f32[4304,40]{0,1:T(8,128)} %fusion.3), channel_id=1, source_target_pairs={{0,1},{1,2},{2,3},{3,4},{4,5},{5,6},{6,7},{7,8},{8,9},{9,10},{10,1... | collective-permute-start | bytes 2065928
  1007.6 70.7 %all-to-all-start.3 = ((bf16[2,576,3,288]{3,0,2,1:T(2,128)(2,1)}), bf16[2,576,3,288]{3,0,2,1:T(2,128)(2,1)}, u32[]{:S(2)}, u32[]{:S(2)}) async-start(bf16[2,576,3,288]{3,0,2,1:T(2,128)(2,1)} %copy.85), calls=%async_computation.3 | async-start | bytes 5308416 | tf_op jit(solution)/shard_map/all_to_all | solution.py:272
  2151.5 54.6 %collective-permute-start.14 = (f32[48,1152]{1,0:T(8,128)S(1)}, f32[48,1152]{1,0:T(8,128)S(1)}, u32[]{:S(2)}, u32[]{:S(2)}) collective-permute-start(f32[48,1152]{1,0:T(8,128)S(1)} %get-tuple-element.212), channel_id=1, source_target_pairs={{0,7},{1,8},{2,9},{3,10},{4,11},{5,12},{6,13},{7,14},{8,15},{9,16}... | collective-permute-start | bytes 663560
  2164.3 107.1 %collective-permute-start.13 = (f32[48,1152]{1,0:T(8,128)S(1)}, f32[48,1152]{1,0:T(8,128)}, u32[]{:S(2)}, u32[]{:S(2)}) collective-permute-start(f32[48,1152]{1,0:T(8,128)S(1)} %get-tuple-element.212), channel_id=1, source_target_pairs={{0,6},{1,7},{2,8},{3,9},{4,10},{5,11},{6,12},{7,13},{8,14},{9,15},... | collective-permute-start | bytes 663560
  2168.7 108.2 %collective-permute-start.12 = (f32[48,1152]{1,0:T(8,128)S(1)}, f32[48,1152]{1,0:T(8,128)}, u32[]{:S(2)}, u32[]{:S(2)}) collective-permute-start(f32[48,1152]{1,0:T(8,128)S(1)} %get-tuple-element.212), channel_id=1, source_target_pairs={{0,5},{1,6},{2,7},{3,8},{4,9},{5,10},{6,11},{7,12},{8,13},{9,14},{... | collective-permute-start | bytes 663560
  2171.5 146.5 %collective-permute-start.6 = (f32[48,3456]{1,0:T(8,128)S(1)}, f32[48,3456]{1,0:T(8,128)S(1)}, u32[]{:S(2)}, u32[]{:S(2)}) collective-permute-start(f32[48,3456]{1,0:T(8,128)S(1)} %get-tuple-element.211), channel_id=1, source_target_pairs={{0,7},{1,8},{2,9},{3,10},{4,11},{5,12},{6,13},{7,14},{8,15},{9,16}... | collective-permute-start | bytes 1990664
  2202.5 123.6 %collective-permute-start.5 = (f32[48,3456]{1,0:T(8,128)S(1)}, f32[48,3456]{1,0:T(8,128)}, u32[]{:S(2)}, u32[]{:S(2)}) collective-permute-start(f32[48,3456]{1,0:T(8,128)S(1)} %get-tuple-element.211), channel_id=1, source_target_pairs={{0,6},{1,7},{2,8},{3,9},{4,10},{5,11},{6,12},{7,13},{8,14},{9,15},... | collective-permute-start | bytes 1990664
  2206.9 98.6 %collective-permute-start.7 = (f32[36,3456]{1,0:T(8,128)}, f32[36,3456]{1,0:T(8,128)}, u32[]{:S(2)}, u32[]{:S(2)}) collective-permute-start(f32[36,3456]{1,0:T(8,128)} %slice.44), channel_id=1, source_target_pairs={{0,8},{1,9},{2,10},{3,11},{4,12},{5,13},{6,14},{7,15},{8,16},{9,17... | collective-permute-start | bytes 1493000
  2299.8 39.7 %collective-permute-start.4 = (f32[48,3456]{1,0:T(8,128)S(1)}, f32[48,3456]{1,0:T(8,128)}, u32[]{:S(2)}, u32[]{:S(2)}) collective-permute-start(f32[48,3456]{1,0:T(8,128)S(1)} %get-tuple-element.211), channel_id=1, source_target_pairs={{0,5},{1,6},{2,7},{3,8},{4,9},{5,10},{6,11},{7,12},{8,13},{9,14},{... | collective-permute-start | bytes 1990664
  2318.0 60.5 %collective-permute-start.1 = (f32[48,3456]{1,0:T(8,128)S(1)}, f32[48,3456]{1,0:T(8,128)}, u32[]{:S(2)}, u32[]{:S(2)}) collective-permute-start(f32[48,3456]{1,0:T(8,128)S(1)} %get-tuple-element.211), channel_id=1, source_target_pairs={{0,2},{1,3},{2,4},{3,5},{4,6},{5,7},{6,8},{7,9},{8,10},{9,11},{10,... | collective-permute-start | bytes 1990664
  2326.2 80.8 %collective-permute-start = (f32[48,3456]{1,0:T(8,128)S(1)}, f32[48,3456]{1,0:T(8,128)}, u32[]{:S(2)}, u32[]{:S(2)}) collective-permute-start(f32[48,3456]{1,0:T(8,128)S(1)} %get-tuple-element.211), channel_id=1, source_target_pairs={{0,1},{1,2},{2,3},{3,4},{4,5},{5,6},{6,7},{7,8},{8,9},{9,10},{10,1... | collective-permute-start | bytes 1990664
  2339.5 106.1 %collective-permute-start.18 = (f32[40,4304]{1,0:T(8,128)S(1)}, f32[40,4304]{1,0:T(8,128)}, u32[]{:S(2)}, u32[]{:S(2)}) collective-permute-start(f32[40,4304]{1,0:T(8,128)S(1)} %copy-done.13), channel_id=1, source_target_pairs={{0,3},{1,4},{2,5},{3,6},{4,7},{5,8},{6,9},{7,10},{8,11},{9,12},{10... | collective-permute-start | bytes 2065928
  2341.5 104.1 %collective-permute-start.17 = (f32[40,4304]{1,0:T(8,128)S(1)}, f32[40,4304]{1,0:T(8,128)}, u32[]{:S(2)}, u32[]{:S(2)}) collective-permute-start(f32[40,4304]{1,0:T(8,128)S(1)} %copy-done.13), channel_id=1, source_target_pairs={{0,2},{1,3},{2,4},{3,5},{4,6},{5,7},{6,8},{7,9},{8,10},{9,11},{10,... | collective-permute-start | bytes 2065928
  2344.0 101.6 %collective-permute-start.16 = (f32[40,4304]{1,0:T(8,128)S(1)}, f32[40,4304]{1,0:T(8,128)}, u32[]{:S(2)}, u32[]{:S(2)}) collective-permute-start(f32[40,4304]{1,0:T(8,128)S(1)} %copy-done.13), channel_id=1, source_target_pairs={{0,1},{1,2},{2,3},{3,4},{4,5},{5,6},{6,7},{7,8},{8,9},{9,10},{10,1... | collective-permute-start | bytes 2065928
  2378.5 67.1 %collective-permute-start.19 = (f32[4,4304]{1,0:T(4,128)}, f32[4,4304]{1,0:T(4,128)S(1)}, u32[]{:S(2)}, u32[]{:S(2)}) collective-permute-start(f32[4,4304]{1,0:T(4,128)} %slice.46), channel_id=1, source_target_pairs={{0,4},{1,5},{2,6},{3,7},{4,8},{5,9},{6,10},{7,11},{8,12},{9,13},{1... | collective-permute-start | bytes 206600
  (56 other events, 6357.1 us)
Sparse Core Ops, SparseCore 0:
  10.8 80.0 all-gather.9
  93.8 56.0 all-gather.11
  152.6 140.3 all-gather.13
  295.7 97.9 all-gather.15
where the time goes:
time: 2480 us; the launch traced here: 2470 us
  blocking collectives  1720 us (69%)
  waiting for transfers between devices  276 us (11%)
  local copies, waits for them, and re-layouts  229 us (9%)
  starting transfers between devices  104 us (4%)
  matrix products  102 us (4%)
    unnamed x4, blocking collectives  1660 us
    unnamed x116, local copies, waits for them, and re-layouts  146 us
    all_to_all x1, waiting for transfers between devices, local(): lax.all_to_all(projected, 'seq', split_axis=3, concat_axis=1, tiled=True)  111 us
    unnamed x28, waiting for transfers between devices  95.3 us
    unnamed x24, starting transfers between devices  78.1 us
    all_gather x1, blocking collectives, local(): lax.all_gather(qv_bias, ('dp', 'seq'), axis=1, tiled=True)  62.3 us
    all_gather x1, waiting for transfers between devices, local(): lax.all_gather(down_weight, ('dp', 'seq'), axis=1, tiled=True)  51.9 us
  transfers between devices with their start and end apart: 32, of which 9 were waited for; matrix products, arithmetic and copies ran while one was open for 31% of the time, Pallas kernels for 0%

commit v1 on v0

--- a/solution.py
+++ b/solution.py
@@ -8,6 +8,22 @@
 EPS = 1e-06
 GELU_C = 0.7978845608028654
 GELU_A = 0.044715
+
+
+def swapped_with_each(x, axis, split, join):
+    ways, here = (lax.axis_size(axis), lax.axis_index(axis))
+    width = x.shape[split] // ways
+    dims = list(x.shape)
+    dims[split] = width
+    height = dims[join]
+    dims[join] = height * ways
+    full = jnp.zeros(dims, x.dtype)
+    for mask in range(ways):
+        part = lax.dynamic_slice_in_dim(x, (here ^ mask) * width, width, axis=split)
+        if mask:
+            part = lax.ppermute(part, axis, [(d, d ^ mask) for d in range(ways)])
+        full = lax.dynamic_update_slice_in_dim(full, part, (here ^ mask) * height, axis=join)
+    return full
 
 
 def layer_norm(values, gain_row, offset):
@@ -163,7 +179,7 @@
         jnp.dot(attn_input, qkv_full, preferred_element_type=jnp.float32) + bias_full
     ).astype(jnp.bfloat16)
     projected = projected.reshape(images, tok_rows, 3, model_width)
-    by_heads = lax.all_to_all(projected, "seq", split_axis=3, concat_axis=1, tiled=True)
+    by_heads = swapped_with_each(projected, "seq", 3, 1)
 
     def attend_one(one_image):
         queries = one_image[:, 0].reshape(length, head_share, HEAD)

time: 2480 us -> 2440 us (0.984)
  waiting for transfers between devices: 276 us -> 186 us
  local copies, waits for them, and re-layouts: 229 us -> 287 us
    all_to_all x1 -> x0, waiting for transfers between devices: 111 us -> none  [local(): lax.all_to_all(projected, 'seq', split_axis=3, concat_axis=1, tiled=True)]
    dynamic_update_slice x0 -> x4, local copies, waits for them, and re-layouts: none -> 67.9 us  [swapped_with_each(): lax.dynamic_update_slice_in_dim(full, part, (here ^ mask) * height, axis=...]
    unnamed x116 -> x120, local copies, waits for them, and re-layouts: 146 us -> 151 us
  transfers between devices with their start and end apart: 32 -> 34, of which waited for: 9 -> 12; matrix products, arithmetic and copies ran while one was open for 31% -> 34% of each run, Pallas kernels for 0% -> 0%
where the time goes in v1:
time: 2440 us; the launch traced here: 2430 us
  blocking collectives  1720 us (70%)
  local copies, waits for them, and re-layouts  287 us (12%)
  waiting for transfers between devices  186 us (8%)
  matrix products  104 us (4%)
  starting transfers between devices  96.5 us (4%)
    unnamed x4, blocking collectives  1660 us
    unnamed x120, local copies, waits for them, and re-layouts  151 us
    unnamed x28, waiting for transfers between devices  105 us
    unnamed x24, starting transfers between devices  76.2 us
    dynamic_update_slice x4, local copies, waits for them, and re-layouts, swapped_with_each(): lax.dynamic_update_slice_in_dim(full, part, (here ^ mask) * height, axis=...  67.9 us
    all_gather x1, blocking collectives, local(): lax.all_gather(qv_bias, ('dp', 'seq'), axis=1, tiled=True)  62.5 us
  transfers between devices with their start and end apart: 34, of which 12 were waited for; matrix products, arithmetic and copies ran while one was open for 34% of the time, Pallas kernels for 0%

profile of v1, /device:TPU:19, one launch (start us, length us, event | category | flops | bytes accessed | tf_op | source)
XLA Modules:
  0.0 2432.1 jit_solution(10180205821874332312)
XLA Ops:
  18.0 41.7 %all-reduce.22 = (bf16[1152]{0:T(1024)(128)(2,1)S(1)}, bf16[1152]{0:T(1024)(128)(2,1)S(1)}, bf16[1152]{0:T(1024)(128)(2,1)}, bf16[1152]{0:T(1024)(128)(2,1)}, bf...) all-reduce(bf16[1152]{0:T(1024)(128)(2,1)S(1)} %dynamic-update-slic, ...), channel_id=1, replica_groups=mesh['dp'=8,'seq'=4] {'dp','seq'}, use_global_device_ids=true, to_apply=%add.1 | all-reduce | flops 6912 | bytes 27648
  59.7 62.5 %all-gather.1 = bf16[32,36,2]{1,2,0:T(2,128)(2,1)S(1)} all-gather(bf16[1,36,2]{1,2,0:T(2,128)(2,1)} %bitcast.192), channel_id=1, replica_groups=mesh['dp'=8,'seq'=4] {'dp','seq'}, dimensions={0}, use_global_device_ids=true | all-gather | bytes 4752 | tf_op jit(solution)/shard_map/all_gather | solution.py:162
  123.8 12.4 reshape.265
  158.7 17.5 dynamic_update_slice.33
  185.0 17.3 dynamic_update_slice.34
  209.1 15.3 dynamic_update_slice.35
  236.0 17.7 dynamic_update_slice.36
  253.7 10.4 while.18
  300.0 14.7 reshape.271
  323.6 9.9 fusion.40
  333.5 37.7 %all-gather.16.cloned.1.call-done = bf16[32,36,4304]{2,1,0:T(8,128)(2,1)} async-done(((bf16[1,36,4304]{2,1,0:T(8,128)(2,1)}), bf16[32,36,4304]{2,1,0:T(8,128)(2,1)}) %all-gather.16.cloned.1.call-update) | async-done | bytes 9916432 | tf_op jit(solution)/shard_map/all_gather | solution.py:208
  371.3 14.4 reshape.273
  417.1 494.5 %fusion.3 = f32[4304,40]{0,1:T(8,128)} fusion(f32[4304,1152]{0,1:T(8,128)} %fusion.40), kind=kCustom, calls=%all-reduce-scatter.3 | all-reduce-scatter fusion | flops 5509121 | bytes 20521472
  933.0 23.9 while.19
  971.1 11.3 fusion.39
  999.7 15.6 concatenate.15
  1016.2 17.1 all-to-all-done.2
  1049.7 1056.8 %fusion.42 = (f32[48,3456]{1,0:T(8,128)S(1)}, f32[48,1152]{1,0:T(8,128)S(1)}, f32[40,4304]{1,0:T(8,128)}) fusion(f32[1152,3456]{1,0:T(8,128)} %fusion.48, f32[1152,1152]{1,0:T(8,128)} %fusion.34, f32[1152,4304]{1,0:T(8,128)} %fusion.39), kind=kCustom, calls=%all-reduce-scatter.4 | all-reduce-scatter fusion | flops 12587010 | bytes 42639872
  2130.5 36.0 %collective-permute-done.18 = f32[36,1152]{1,0:T(8,128)S(1)} collective-permute-done((f32[36,1152]{1,0:T(8,128)S(1)}, f32[36,1152]{1,0:T(8,128)S(1)}, u32[]{:S(2)}, u32[]{:S(2)}) %collective-permute-start.18) | collective-permute-done | bytes 165920
  2171.7 63.4 %all-reduce.21 = (f32[1152]{0:T(1024)}, f32[1152]{0:T(1024)}, f32[2,1152]{1,0:T(2,128)}, f32[1152]{0:T(1024)}, f32[1152]{0:T(1024)}, /*index=5*/f32[1152]{0:T(1024)}, f32[4304]{0:T(1024)}, f32[1152]{0:T(1024)}) all-reduce(f32[1152]{0:T(1024)} %get-tuple-element.153, ...), channel_id=2, replica_groups=mesh['dp'=8,'seq'=4] {'dp','seq'}, use_global_device_ids=true, to_apply=%region_16.17.clone | all-reduce | flops 13520 | bytes 108160
  2311.0 31.4 %collective-permute-done.4 = f32[48,3456]{1,0:T(8,128)} collective-permute-done((f32[48,3456]{1,0:T(8,128)S(1)}, f32[48,3456]{1,0:T(8,128)}, u32[]{:S(2)}, u32[]{:S(2)}) %collective-permute-start.4) | collective-permute-done | bytes 663584
  2344.4 26.5 %collective-permute-done.3 = f32[48,3456]{1,0:T(8,128)} collective-permute-done((f32[48,3456]{1,0:T(8,128)S(1)}, f32[48,3456]{1,0:T(8,128)}, u32[]{:S(2)}, u32[]{:S(2)}) %collective-permute-start.3) | collective-permute-done | bytes 663584
  2370.9 36.8 %concatenate.12 = f32[420,3456]{1,0:T(8,128)} concatenate(f32[36,3456]{1,0:T(8,128)} %collective-permute-done.10, f32[48,3456]{1,0:T(8,128)} %copy-done.22, f32[48,3456]{1,0:T(8,128)} %collective-permute-done.8, f32[48,3456]{1,0:T(8,128)} %collective-permute-done.7, f32[48,3456]{1,0:T(8,128)} %collective-permute-done.6, f32[48,3456]{1,0:T(8,128)} %collective-permute-done.5, ...), dimensions={0} | concatenate | bytes 11612160
  2409.6 14.5 concatenate.14
  (299 shorter events, 351.2 us)
Async XLA Ops:
  7.2 116.6 %all-gather.10.cloned.1.call-start = ((), (), s32[]{:S(2)}) async-start(), calls=%async_computation.3 | async-start | bytes 9123840 | tf_op jit(solution)/shard_map/all_gather | solution.py:161
  7.9 270.8 %all-gather.12.cloned.1.call-start = ((), (), s32[]{:S(2)}) async-start(), calls=%async_computation.4 | async-start | bytes 3041280 | tf_op jit(solution)/shard_map/all_gather | solution.py:163
  8.7 291.3 %all-gather.14.cloned.1.call-start = ((), (), s32[]{:S(2)}) async-start(), calls=%async_computation.5 | async-start | bytes 11489280 | tf_op jit(solution)/shard_map/all_gather | solution.py:207
  9.4 361.8 %all-gather.16.cloned.1.call-start = ((), (), s32[]{:S(2)}) async-start(), calls=%async_computation.6 | async-start | bytes 11489280 | tf_op jit(solution)/shard_map/all_gather | solution.py:208
  155.8 50.9 %collective-permute-start.1 = (bf16[2,144,3,288]{3,1,2,0:T(8,128)(2,1)}, bf16[2,144,3,288]{3,1,2,0:T(8,128)(2,1)}, u32[]{:S(2)}, u32[]{:S(2)}) collective-permute-start(bf16[2,144,3,288]{3,1,2,0:T(8,128)(2,1)} %copy.81), channel_id=1, source_target_pairs={{0,2},{1,3},{2,0},{3,1},{4,6},{5,7},{6,4},{7,5},{8,10},{9,11},{10,... | collective-permute-start | bytes 1493000 | tf_op jit(solution)/shard_map/ppermute | solution.py:24
  155.8 77.8 %collective-permute-start.2 = (bf16[2,144,3,288]{3,1,2,0:T(8,128)(2,1)S(1)}, bf16[2,144,3,288]{3,1,2,0:T(8,128)(2,1)}, u32[]{:S(2)}, u32[]{:S(2)}) collective-permute-start(bf16[2,144,3,288]{3,1,2,0:T(8,128)(2,1)S(1)} %copy.83), channel_id=1, source_target_pairs={{0,3},{1,2},{2,1},{3,0},{4,7},{5,6},{6,5},{7,4},{8,11},{9,10},{10,... | collective-permute-start | bytes 1493000 | tf_op jit(solution)/shard_map/ppermute | solution.py:24
  412.1 510.1 %all-to-all-start.1 = ((bf16[2,144,1152]{1,0,2:T(2,128)(2,1)}), bf16[2,144,1152]{1,0,2:T(2,128)(2,1)}, u32[]{:S(2)}, u32[]{:S(2)}) async-start(bf16[2,144,1152]{1,0,2:T(2,128)(2,1)} %copy.88), calls=%async_computation.1 | async-start | bytes 2359296 | tf_op jit(solution)/shard_map/all_to_all | solution.py:266
  911.6 87.5 %collective-permute-start.25 = (f32[4304,40]{0,1:T(8,128)}, f32[4304,40]{0,1:T(8,128)}, u32[]{:S(2)}, u32[]{:S(2)}) collective-permute-start(f32[4304,40]{0,1:T(8,128)} %fusion.3), channel_id=1, source_target_pairs={{0,3},{1,4},{2,5},{3,6},{4,7},{5,8},{6,9},{7,10},{8,11},{9,12},{10... | collective-permute-start | bytes 2065928
  916.0 83.1 %collective-permute-start.24 = (f32[4304,40]{0,1:T(8,128)}, f32[4304,40]{0,1:T(8,128)}, u32[]{:S(2)}, u32[]{:S(2)}) collective-permute-start(f32[4304,40]{0,1:T(8,128)} %fusion.3), channel_id=1, source_target_pairs={{0,2},{1,3},{2,4},{3,5},{4,6},{5,7},{6,8},{7,9},{8,10},{9,11},{10,... | collective-permute-start | bytes 2065928
  920.3 79.4 %collective-permute-start.23 = (f32[4304,40]{0,1:T(8,128)}, f32[4304,40]{0,1:T(8,128)}, u32[]{:S(2)}, u32[]{:S(2)}) collective-permute-start(f32[4304,40]{0,1:T(8,128)} %fusion.3), channel_id=1, source_target_pairs={{0,1},{1,2},{2,3},{3,4},{4,5},{5,6},{6,7},{7,8},{8,9},{9,10},{10,1... | collective-permute-start | bytes 2065928
  964.0 69.3 %all-to-all-start.2 = ((bf16[2,576,3,288]{3,0,2,1:T(2,128)(2,1)}), bf16[2,576,3,288]{3,0,2,1:T(2,128)(2,1)}, u32[]{:S(2)}, u32[]{:S(2)}) async-start(bf16[2,576,3,288]{3,0,2,1:T(2,128)(2,1)} %copy.92), calls=%async_computation.2 | async-start | bytes 5308416 | tf_op jit(solution)/shard_map/all_to_all | solution.py:288
  2106.5 62.0 %collective-permute-start.17 = (f32[48,1152]{1,0:T(8,128)S(1)}, f32[48,1152]{1,0:T(8,128)S(1)}, u32[]{:S(2)}, u32[]{:S(2)}) collective-permute-start(f32[48,1152]{1,0:T(8,128)S(1)} %get-tuple-element.196), channel_id=1, source_target_pairs={{0,7},{1,8},{2,9},{3,10},{4,11},{5,12},{6,13},{7,14},{8,15},{9,16}... | collective-permute-start | bytes 663560
  2119.3 115.7 %collective-permute-start.16 = (f32[48,1152]{1,0:T(8,128)S(1)}, f32[48,1152]{1,0:T(8,128)}, u32[]{:S(2)}, u32[]{:S(2)}) collective-permute-start(f32[48,1152]{1,0:T(8,128)S(1)} %get-tuple-element.196), channel_id=1, source_target_pairs={{0,6},{1,7},{2,8},{3,9},{4,10},{5,11},{6,12},{7,13},{8,14},{9,15},... | collective-permute-start | bytes 663560
  2123.7 117.1 %collective-permute-start.15 = (f32[48,1152]{1,0:T(8,128)S(1)}, f32[48,1152]{1,0:T(8,128)}, u32[]{:S(2)}, u32[]{:S(2)}) collective-permute-start(f32[48,1152]{1,0:T(8,128)S(1)} %get-tuple-element.196), channel_id=1, source_target_pairs={{0,5},{1,6},{2,7},{3,8},{4,9},{5,10},{6,11},{7,12},{8,13},{9,14},{... | collective-permute-start | bytes 663560
  2126.5 155.2 %collective-permute-start.9 = (f32[48,3456]{1,0:T(8,128)S(1)}, f32[48,3456]{1,0:T(8,128)S(1)}, u32[]{:S(2)}, u32[]{:S(2)}) collective-permute-start(f32[48,3456]{1,0:T(8,128)S(1)} %get-tuple-element.195), channel_id=1, source_target_pairs={{0,7},{1,8},{2,9},{3,10},{4,11},{5,12},{6,13},{7,14},{8,15},{9,16}... | collective-permute-start | bytes 1990664
  2166.5 123.4 %collective-permute-start.8 = (f32[48,3456]{1,0:T(8,128)S(1)}, f32[48,3456]{1,0:T(8,128)}, u32[]{:S(2)}, u32[]{:S(2)}) collective-permute-start(f32[48,3456]{1,0:T(8,128)S(1)} %get-tuple-element.195), channel_id=1, source_target_pairs={{0,6},{1,7},{2,8},{3,9},{4,10},{5,11},{6,12},{7,13},{8,14},{9,15},... | collective-permute-start | bytes 1990664
  2169.2 100.1 %collective-permute-start.10 = (f32[36,3456]{1,0:T(8,128)}, f32[36,3456]{1,0:T(8,128)}, u32[]{:S(2)}, u32[]{:S(2)}) collective-permute-start(f32[36,3456]{1,0:T(8,128)} %slice.44), channel_id=1, source_target_pairs={{0,8},{1,9},{2,10},{3,11},{4,12},{5,13},{6,14},{7,15},{8,16},{9,17... | collective-permute-start | bytes 1493000
  2263.8 39.5 %collective-permute-start.7 = (f32[48,3456]{1,0:T(8,128)S(1)}, f32[48,3456]{1,0:T(8,128)}, u32[]{:S(2)}, u32[]{:S(2)}) collective-permute-start(f32[48,3456]{1,0:T(8,128)S(1)} %get-tuple-element.195), channel_id=1, source_target_pairs={{0,5},{1,6},{2,7},{3,8},{4,9},{5,10},{6,11},{7,12},{8,13},{9,14},{... | collective-permute-start | bytes 1990664
  2281.7 60.7 %collective-permute-start.4 = (f32[48,3456]{1,0:T(8,128)S(1)}, f32[48,3456]{1,0:T(8,128)}, u32[]{:S(2)}, u32[]{:S(2)}) collective-permute-start(f32[48,3456]{1,0:T(8,128)S(1)} %get-tuple-element.195), channel_id=1, source_target_pairs={{0,2},{1,3},{2,4},{3,5},{4,6},{5,7},{6,8},{7,9},{8,10},{9,11},{10,... | collective-permute-start | bytes 1990664
  2289.9 81.0 %collective-permute-start.3 = (f32[48,3456]{1,0:T(8,128)S(1)}, f32[48,3456]{1,0:T(8,128)}, u32[]{:S(2)}, u32[]{:S(2)}) collective-permute-start(f32[48,3456]{1,0:T(8,128)S(1)} %get-tuple-element.195), channel_id=1, source_target_pairs={{0,1},{1,2},{2,3},{3,4},{4,5},{5,6},{6,7},{7,8},{8,9},{9,10},{10,1... | collective-permute-start | bytes 1990664
  2303.4 106.2 %collective-permute-start.21 = (f32[40,4304]{1,0:T(8,128)S(1)}, f32[40,4304]{1,0:T(8,128)}, u32[]{:S(2)}, u32[]{:S(2)}) collective-permute-start(f32[40,4304]{1,0:T(8,128)S(1)} %copy-done.19), channel_id=1, source_target_pairs={{0,3},{1,4},{2,5},{3,6},{4,7},{5,8},{6,9},{7,10},{8,11},{9,12},{10... | collective-permute-start | bytes 2065928
  2305.3 104.3 %collective-permute-start.20 = (f32[40,4304]{1,0:T(8,128)S(1)}, f32[40,4304]{1,0:T(8,128)}, u32[]{:S(2)}, u32[]{:S(2)}) collective-permute-start(f32[40,4304]{1,0:T(8,128)S(1)} %copy-done.19), channel_id=1, source_target_pairs={{0,2},{1,3},{2,4},{3,5},{4,6},{5,7},{6,8},{7,9},{8,10},{9,11},{10,... | collective-permute-start | bytes 2065928
  2307.8 101.8 %collective-permute-start.19 = (f32[40,4304]{1,0:T(8,128)S(1)}, f32[40,4304]{1,0:T(8,128)}, u32[]{:S(2)}, u32[]{:S(2)}) collective-permute-start(f32[40,4304]{1,0:T(8,128)S(1)} %copy-done.19), channel_id=1, source_target_pairs={{0,1},{1,2},{2,3},{3,4},{4,5},{5,6},{6,7},{7,8},{8,9},{9,10},{10,1... | collective-permute-start | bytes 2065928
  2342.4 67.2 %collective-permute-start.22 = (f32[4,4304]{1,0:T(4,128)}, f32[4,4304]{1,0:T(4,128)S(1)}, u32[]{:S(2)}, u32[]{:S(2)}) collective-permute-start(f32[4,4304]{1,0:T(4,128)} %slice.46), channel_id=1, source_target_pairs={{0,4},{1,5},{2,6},{3,7},{4,8},{5,9},{6,10},{7,11},{8,12},{9,13},{1... | collective-permute-start | bytes 206600
  (60 other events, 6338.4 us)
Sparse Core Ops, SparseCore 0:
  10.8 80.0 all-gather.9
  93.7 55.9 all-gather.11
  152.6 126.0 all-gather.13
  281.4 89.8 all-gather.15
